TPU v7x, 256 devices: a whole 4x4x8 slice. The times are simulated.
256 devices in a mesh: group: 32 (over z, x), member: 4 (over y), pair: 2 (over core).
Axes of the slice: x: 4, y: 4, z: 8, core: 2. Of those that a mesh axis runs over, the one named last changes fastest.
Arguments:
- tokens: bfloat16 [32768, 768], P(('group', 'member', 'pair')), may hold values from -6 to 6
- out_grad: bfloat16 [32768, 768], P(('group', 'member', 'pair')), may hold values from -6 to 6
- router_gate: float32 [32768], P(('group', 'member', 'pair')), may hold values from 0.2 to 1
- expand_weight: bfloat16 [128, 768, 3072], P(('group', 'member'), None, 'pair'), may hold values from -0.21875 to 0.21875
- shrink_weight: bfloat16 [128, 3072, 768], P(('group', 'member'), 'pair'), may hold values from -0.109375 to 0.109375
- expert_ids: int32 [32768], P(('group', 'member', 'pair')), may hold values from 0 to 127, as said below
- slot_ids: int32 [32768], P(('group', 'member', 'pair')), may hold values from 0 to 1, as said below
- capacity: int32 [128], replicated, may hold values from 1 to 2, as said below
Outputs:
- token_grad: bfloat16 [32768, 768], P(('group', 'member', 'pair'))
- expand_grad: bfloat16 [128, 768, 3072], P(('group', 'member'), None, 'pair')
- shrink_grad: bfloat16 [128, 3072, 768], P(('group', 'member'), 'pair')
Inputs may be any that keep to these rules, and one draw needn't show every extreme that they name: `expert_ids`: in each aligned block of 128 tokens (the tokens of one device) no expert is named by more than 2 tokens, and one expert, the same for all blocks, is named by exactly 2 tokens in every block. `slot_ids`: A token's slot is the number of earlier tokens of its aligned block of 128 that name the same expert. The expert that is named 2 times in every block has capacity 2.
All inputs are finite; a program needn't handle non-finite values.
Results may differ from a plain program's by a relative error of at most 0.0058.
Values may be sent and summed in bfloat16 or wider, within the bound.
A program may use at most 64 MiB of HBM per device.

v0:
```python
import jax
import jax.numpy as jnp
from jax import lax
from jax.sharding import PartitionSpec as P


def activation(value):
    return jax.nn.gelu(value, approximate=True)


def expert_pass(token_rows, grad_rows, expand_local, shrink_local):
    preact = jnp.einsum(
        "plrd,ldf->plrf", token_rows, expand_local, preferred_element_type=jnp.float32
    )
    hidden, pullback = jax.vjp(activation, preact)
    hidden_low = hidden.astype(jnp.bfloat16)
    post_grad = jnp.einsum(
        "plrd,lfd->plrf", grad_rows, shrink_local, preferred_element_type=jnp.float32
    )
    pre_grad = pullback(post_grad)[0].astype(jnp.bfloat16)
    expand_part = jnp.einsum(
        "plrd,plrf->ldf", token_rows, pre_grad, preferred_element_type=jnp.float32
    ).astype(jnp.bfloat16)
    shrink_part = jnp.einsum(
        "plrf,plrd->lfd", hidden_low, grad_rows, preferred_element_type=jnp.float32
    ).astype(jnp.bfloat16)
    partial_value = jnp.einsum(
        "plrf,ldf->plrd", pre_grad, expand_local, preferred_element_type=jnp.float32
    )
    return (expand_part, shrink_part, partial_value)


def per_device(
    tokens, out_grad, router_gate, expand_weight, shrink_weight, expert_ids, slot_ids, capacity
):
    tok_dev, model_width = tokens.shape
    expert_count = capacity.shape[0]
    slot_count = max(2, 2 * tok_dev // expert_count)
    expert_table = jnp.arange(expert_count, dtype=jnp.int32)
    matches = expert_ids[:, None] == expert_table[None, :]
    limits = jnp.sum(jnp.where(matches, capacity[None, :], 0), axis=1)
    keep_mask = slot_ids < limits
    target = jnp.where(keep_mask, expert_ids * slot_count + slot_ids, expert_count * slot_count)
    scaled = (router_gate[:, None] * out_grad.astype(jnp.float32)).astype(jnp.bfloat16)
    token_send = (
        jnp.zeros((expert_count * slot_count, model_width), jnp.bfloat16)
        .at[target]
        .set(tokens, mode="drop")
    )
    grad_send = (
        jnp.zeros((expert_count * slot_count, model_width), jnp.bfloat16)
        .at[target]
        .set(scaled, mode="drop")
    )
    token_send = token_send.reshape(1, expert_count, slot_count, model_width)
    grad_send = grad_send.reshape(1, expert_count, slot_count, model_width)
    token_both, grad_both = (
        lax.all_gather(token_send, "pair", axis=0, tiled=True),
        lax.all_gather(grad_send, "pair", axis=0, tiled=True),
    )
    token_rows, grad_rows = (
        lax.all_to_all(token_both, ("group", "member"), split_axis=1, concat_axis=2, tiled=True),
        lax.all_to_all(grad_both, ("group", "member"), split_axis=1, concat_axis=2, tiled=True),
    )
    expand_grad, shrink_grad, partial_value = expert_pass(
        token_rows, grad_rows, expand_weight, shrink_weight
    )
    returned = lax.all_to_all(
        partial_value, ("group", "member"), split_axis=2, concat_axis=1, tiled=True
    )
    summed = lax.psum_scatter(returned, "pair", scatter_dimension=0, tiled=True).astype(
        jnp.bfloat16
    )
    flattened = summed.reshape(expert_count * slot_count, model_width)
    picked = flattened[jnp.minimum(target, expert_count * slot_count - 1)]
    token_grad = jnp.where(keep_mask[:, None], picked, jnp.zeros((), jnp.bfloat16))
    return (token_grad, expand_grad, shrink_grad)


def solution(mesh):
    placed = (
        P(("group", "member", "pair"), None),
        P(("group", "member", "pair"), None),
        P(("group", "member", "pair")),
        P(("group", "member"), None, "pair"),
        P(("group", "member"), "pair", None),
        P(("group", "member", "pair")),
        P(("group", "member", "pair")),
        P(),
    )
    return jax.shard_map(
        per_device,
        mesh=mesh,
        in_specs=placed,
        out_specs=(
            P(("group", "member", "pair"), None),
            P(("group", "member"), None, "pair"),
            P(("group", "member"), "pair", None),
        ),
        check_vma=False,
    )
```

profile of v0, /device:TPU:1, one launch (start us, length us, event | category | flops | bytes accessed | tf_op | source)
XLA Modules:
  0.0 166.8 jit_solution(89248312852301945)
XLA Ops:
  7.2 0.0 copy-start
  7.2 1.0 select_reduce_fusion
  8.2 0.7 compare_select_fusion
  8.9 0.0 copy-start.4
  8.9 1.6 scatter_custom_fusion.1
  10.5 0.1 reshape.64
  10.7 5.2 %all_gather.7 = bf16[2,128,2,768]{3,1,2,0:T(8,128)(2,1)S(1)} all-gather(bf16[1,128,2,768]{3,1,2,0:T(8,128)(2,1)S(1)} %copy.29), channel_id=1, replica_groups=mesh['group'=32,'member'=4,'pair'=2] {'pair'}, dimensions={0}, use_global_device_ids=true | all-gather | bytes 1179648 | tf_op jit(solution)/shard_map/all_gather | solution.py:58
  16.0 1.7 %copy.30 = bf16[2,128,2,768]{3,2,0,1:T(2,128)(2,1)} copy(bf16[2,128,2,768]{3,1,2,0:T(8,128)(2,1)S(1)} %all_gather.7) | data formatting | bytes 1572864 | tf_op jit(solution)/shard_map/all_gather | solution.py:58
  17.7 13.8 %all-to-all-start.1 = ((bf16[2,128,2,768]{3,2,0,1:T(2,128)(2,1)}), bf16[2,128,2,768]{3,2,0,1:T(2,128)(2,1)S(1)}, u32[]{:S(2)}, u32[]{:S(2)}) async-start(bf16[2,128,2,768]{3,2,0,1:T(2,128)(2,1)} %copy.30), calls=%async_computation.1 | async-start | bytes 1572864 | tf_op jit(solution)/shard_map/all_to_all | solution.py:62
  31.4 0.0 copy-done.4
  31.4 1.7 %scatter_custom_fusion = bf16[256,768]{1,0:T(8,128)(2,1)S(1)} fusion(s32[128]{0:T(128)S(1)} %compare_select_fusion.1, bf16[128,768]{1,0:T(8,128)(2,1)} %param.9, f32[128]{0:T(128)S(1)} %copy-done.4, bf16[]{:T(256)} %constant.12.clone.1), kind=kCustom, calls=%fused_computation.30 | custom fusion | flops 294912 | bytes 590338 | tf_op jit(solution)/shard_map/scatter | solution.py:53
  33.2 0.9 reshape.61
  34.1 1.0 copy.26
  35.1 2.6 %all_gather.6 = bf16[2,128,2,768]{3,1,2,0:T(8,128)(2,1)S(1)} all-gather(bf16[1,128,2,768]{3,1,2,0:T(8,128)(2,1)S(1)} %copy.26), channel_id=1, replica_groups=mesh['group'=32,'member'=4,'pair'=2] {'pair'}, dimensions={0}, use_global_device_ids=true | all-gather | bytes 1179648 | tf_op jit(solution)/shard_map/all_gather | solution.py:59
  37.7 1.7 %copy.27 = bf16[2,128,2,768]{3,2,0,1:T(2,128)(2,1)} copy(bf16[2,128,2,768]{3,1,2,0:T(8,128)(2,1)S(1)} %all_gather.6) | data formatting | bytes 1572864 | tf_op jit(solution)/shard_map/all_gather | solution.py:59
  39.5 16.0 %all-to-all-done.1 = bf16[2,128,2,768]{3,2,0,1:T(2,128)(2,1)S(1)} async-done(((bf16[2,128,2,768]{3,2,0,1:T(2,128)(2,1)}), bf16[2,128,2,768]{3,2,0,1:T(2,128)(2,1)S(1)}, u32[]{:S(2)}, u32[]{:S(2)}) %all-to-all-start.1) | async-done | bytes 786464 | tf_op jit(solution)/shard_map/all_to_all | solution.py:62
  55.4 7.7 %all-to-all-start = ((bf16[2,128,2,768]{3,2,0,1:T(2,128)(2,1)}), bf16[2,128,2,768]{3,2,0,1:T(2,128)(2,1)}, u32[]{:S(2)}, u32[]{:S(2)}) async-start(bf16[2,128,2,768]{3,2,0,1:T(2,128)(2,1)} %copy.27), calls=%async_computation | async-start | bytes 1572864 | tf_op jit(solution)/shard_map/all_to_all | solution.py:63
  63.1 0.2 reduce-scatter.2.cloned.1.call-start
  63.3 1.4 copy.31
  64.8 3.0 %reshape.65 = bf16[2,256,768]{2,1,0:T(8,128)(2,1)} reshape(bf16[2,128,2,768]{3,2,1,0:T(2,128)(2,1)} %copy.31) | data formatting | bytes 1572864 | tf_op jit(solution)/shard_map/reshape.14
  67.7 17.0 %all-to-all-done = bf16[2,128,2,768]{3,2,0,1:T(2,128)(2,1)} async-done(((bf16[2,128,2,768]{3,2,0,1:T(2,128)(2,1)}), bf16[2,128,2,768]{3,2,0,1:T(2,128)(2,1)}, u32[]{:S(2)}, u32[]{:S(2)}) %all-to-all-start) | async-done | bytes 786464 | tf_op jit(solution)/shard_map/all_to_all | solution.py:63
  84.7 1.7 %copy.28 = bf16[2,128,2,768]{3,2,1,0:T(2,128)(2,1)S(1)} copy(bf16[2,128,2,768]{3,2,0,1:T(2,128)(2,1)} %all-to-all-done) | data formatting | bytes 1572864 | tf_op jit(solution)/shard_map/all_to_all | solution.py:63
  86.4 1.2 reshape.62
  87.6 0.0 copy-done
  87.6 2.7 %convolution_bitcast_fusion = f32[2,1,256,1536]{3,2,0,1:T(8,128)S(1)} fusion(bf16[2,256,768]{2,1,0:T(8,128)(2,1)} %reshape.65, bf16[1,768,1536]{2,1,0:T(8,128)(2,1)S(1)} %copy-done), kind=kOutput, calls=%fused_computation.7 | convolution fusion | flops 1207959552 | bytes 6291456 | tf_op jit(solution)/shard_map/plrd,ldf->plrf/dot_general | solution.py:12
  90.2 0.0 copy-done.2
  90.3 0.0 copy-done.5
  90.3 0.0 copy-start.6
  90.3 3.0 %fusion.9 = bf16[2,256,1536]{2,1,0:T(8,128)(2,1)S(1)} fusion(f32[2,1,256,1536]{3,2,0,1:T(8,128)S(1)} %convolution_bitcast_fusion, bf16[2,256,768]{2,1,0:T(8,128)(2,1)S(1)} %copy-done.2, bf16[1,1536,768]{2,1,0:T(8,128)(2,1)S(1)} %copy-done.5), kind=kOutput, calls=%fused_computation.19 | convolution fusion | flops 1223688192 | bytes 7864320 | tf_op jit(solution)/shard_map/plrd,lfd->plrf/dot_general | solution.py:17
  93.3 0.0 copy-done.6
  93.3 0.0 copy-start.8
  93.3 1.4 fusion.18
  94.8 1.2 copy.32
  96.0 44.8 %all_to_all.30 = f32[2,1,256,768]{3,0,1,2:T(2,128)S(1)} all-to-all(f32[2,1,256,768]{3,0,1,2:T(2,128)S(1)} %copy.32), channel_id=1, replica_groups=mesh['group'=32,'member'=4,'pair'=2] {'group','member'}, dimensions={2} | all-to-all | bytes 3145728 | tf_op jit(solution)/shard_map/all_to_all | solution.py:68
  140.8 1.4 copy.33
  142.2 0.0 reduce-scatter.2.cloned.1.call-update
  142.3 0.0 copy-done.1
  142.3 0.0 copy-start.3
  142.3 0.0 copy-start.7
  142.3 4.4 %fusion.7 = bf16[1,768,1536]{2,1,0:T(8,128)(2,1)} fusion(bf16[2,256,768]{2,1,0:T(8,128)(2,1)S(1)} %copy-done.1, bf16[2,256,1536]{2,1,0:T(8,128)(2,1)} %copy-done.8), kind=kOutput, calls=%fused_computation.17 | convolution fusion | flops 1209139200 | bytes 4718592 | tf_op jit(solution)/shard_map/plrd,plrf->ldf/dot_general | solution.py:21
  146.7 0.0 copy-done.7
  146.7 3.1 %fusion.8 = bf16[1,1536,768]{2,1,0:T(8,128)(2,1)} fusion(bf16[2,256,768]{2,1,0:T(8,128)(2,1)S(1)} %copy-done.3, f32[2,1,256,1536]{3,2,0,1:T(8,128)S(1)} %copy-done.7), kind=kOutput, calls=%fused_computation.18 | convolution fusion | flops 1216217088 | bytes 6291456 | tf_op jit(solution)/shard_map/plrf,plrd->lfd/dot_general | solution.py:24
  149.8 6.7 %reduce-scatter.2.cloned.1.call-done = f32[1,128,2,768]{3,1,2,0:T(8,128)} async-done(((f32[2,128,2,768]{3,1,2,0:T(8,128)}), f32[1,128,2,768]{3,1,2,0:T(8,128)}) %reduce-scatter.2.cloned.1.call-update) | async-done | bytes 786448 | tf_op jit(solution)/shard_map/reduce_scatter | solution.py:71
  156.5 1.2 convert_element_type.30
  157.7 0.4 copy.34
  158.1 0.1 reshape.68
  158.3 0.9 gather_fusion
  159.2 0.8 broadcast_select_fusion
  (8 shorter events, 0.1 us)
Async XLA Ops:
  7.2 80.4 %copy-start = (bf16[1,768,1536]{2,1,0:T(8,128)(2,1)S(1)}, bf16[1,768,1536]{2,1,0:T(8,128)(2,1)}, u32[]{:S(2)}) copy-start(bf16[1,768,1536]{2,1,0:T(8,128)(2,1)} %param.11) | copy-start | bytes 7077892
  8.9 22.6 %copy-start.4 = (f32[128]{0:T(128)S(1)}, f32[128]{0:T(128)}, u32[]{:S(2)}) copy-start(f32[128]{0:T(128)} %param.10) | copy-start | bytes 1540
  17.7 37.8 %all-to-all-start.1 = ((bf16[2,128,2,768]{3,2,0,1:T(2,128)(2,1)}), bf16[2,128,2,768]{3,2,0,1:T(2,128)(2,1)S(1)}, u32[]{:S(2)}, u32[]{:S(2)}) async-start(bf16[2,128,2,768]{3,2,0,1:T(2,128)(2,1)} %copy.30), calls=%async_computation.1 | async-start | bytes 1572864 | tf_op jit(solution)/shard_map/all_to_all | solution.py:62
  55.4 29.3 %all-to-all-start = ((bf16[2,128,2,768]{3,2,0,1:T(2,128)(2,1)}), bf16[2,128,2,768]{3,2,0,1:T(2,128)(2,1)}, u32[]{:S(2)}, u32[]{:S(2)}) async-start(bf16[2,128,2,768]{3,2,0,1:T(2,128)(2,1)} %copy.27), calls=%async_computation | async-start | bytes 1572864 | tf_op jit(solution)/shard_map/all_to_all | solution.py:63
  63.1 93.4 %reduce-scatter.2.cloned.1.call-start = ((), (), s32[]{:S(2)}) async-start(), calls=%async_computation.4 | async-start | bytes 2359296 | tf_op jit(solution)/shard_map/reduce_scatter | solution.py:71
  87.6 2.7 %copy-start.2 = (bf16[2,256,768]{2,1,0:T(8,128)(2,1)S(1)}, bf16[2,256,768]{2,1,0:T(8,128)(2,1)}, u32[]{:S(2)}) copy-start(bf16[2,256,768]{2,1,0:T(8,128)(2,1)} %reshape.62) | copy-start | bytes 2359300
  87.6 2.7 %copy-start.5 = (bf16[1,1536,768]{2,1,0:T(8,128)(2,1)S(1)}, bf16[1,1536,768]{2,1,0:T(8,128)(2,1)}, u32[]{:S(2)}) copy-start(bf16[1,1536,768]{2,1,0:T(8,128)(2,1)} %param.12) | copy-start | bytes 7077892
  90.3 3.1 %copy-start.6 = (f32[2,1,256,1536]{3,2,0,1:T(8,128)}, f32[2,1,256,1536]{3,2,0,1:T(8,128)S(1)}, u32[]{:S(2)}) copy-start(f32[2,1,256,1536]{3,2,0,1:T(8,128)S(1)} %convolution_bitcast_fusion) | copy-start | bytes 9437188
  93.3 1.4 copy-start.8
  140.8 1.5 copy-start.1
  142.3 4.4 %copy-start.3 = (bf16[2,256,768]{2,1,0:T(8,128)(2,1)S(1)}, bf16[2,256,768]{2,1,0:T(8,128)(2,1)}, u32[]{:S(2)}) copy-start(bf16[2,256,768]{2,1,0:T(8,128)(2,1)} %reshape.62) | copy-start | bytes 2359300
  142.3 4.4 %copy-start.7 = (f32[2,1,256,1536]{3,2,0,1:T(8,128)S(1)}, f32[2,1,256,1536]{3,2,0,1:T(8,128)}, u32[]{:S(2)}) copy-start(f32[2,1,256,1536]{3,2,0,1:T(8,128)} %copy-done.6) | copy-start | bytes 9437188
Sparse Core Ops, SparseCore 0:
  142.4 14.1 reduce-scatter.1
where the time goes:
time: 167 us
  blocking collectives  52.7 us (32%)
  waiting for transfers between devices  39.7 us (24%)
  starting transfers between devices  21.7 us (13%)
  local copies, waits for them, and re-layouts  18.5 us (11%)
  matrix products  14.6 us (9%)
  between operations  14.2 us (9%)
  other arithmetic  5.33 us (3%)
    all_to_all x1, blocking collectives, per_device(): lax.all_to_all(partial_value, ('group', 'member'), split_axis=2, concat_a...  44.8 us
    all_to_all x1, waiting for transfers between devices, per_device(): lax.all_to_all(grad_both, ('group', 'member'), split_axis=1, concat_axis=...  17 us
    all_to_all x1, waiting for transfers between devices, per_device(): lax.all_to_all(token_both, ('group', 'member'), split_axis=1, concat_axis...  16 us
    all_to_all x1, starting transfers between devices, per_device(): lax.all_to_all(token_both, ('group', 'member'), split_axis=1, concat_axis...  13.8 us
    all_to_all x1, starting transfers between devices, per_device(): lax.all_to_all(grad_both, ('group', 'member'), split_axis=1, concat_axis=...  7.67 us
    reduce_scatter x1, waiting for transfers between devices, per_device(): lax.psum_scatter(returned, 'pair', scatter_dimension=0, tiled=True)  6.7 us
    all_gather x1, blocking collectives, per_device(): lax.all_gather(token_send, 'pair', axis=0, tiled=True)  5.24 us
    dot_general x1, matrix products, expert_pass(): jnp.einsum('plrd,plrf->ldf', token_rows, pre_grad, preferred_element_type...  4.38 us
  transfers between devices with their start and end apart: 3, of which 3 were waited for; matrix products, arithmetic and copies ran while one was open for 10% of the time, Pallas kernels for 0%

commit v1 on v0

v1 whole, which is shorter than its diff:
```python
import jax
import jax.numpy as jnp
from jax import lax
from jax.sharding import PartitionSpec as P


def activation(value):
    return jax.nn.gelu(value, approximate=True)


def expert_pass(token_rows, grad_rows, expand, shrink):
    f32 = jnp.float32
    preact = jnp.einsum("rd,df->rf", token_rows, expand, preferred_element_type=f32)
    hidden, pullback = jax.vjp(activation, preact)
    hidden_low = hidden.astype(jnp.bfloat16)
    post_grad = jnp.einsum("rd,fd->rf", grad_rows, shrink, preferred_element_type=f32)
    pre_grad = pullback(post_grad)[0].astype(jnp.bfloat16)
    partial_value = jnp.einsum("rf,df->rd", pre_grad, expand, preferred_element_type=f32)
    expand_part = jnp.einsum("rd,rf->df", token_rows, pre_grad, preferred_element_type=f32)
    shrink_part = jnp.einsum("rf,rd->fd", hidden_low, grad_rows, preferred_element_type=f32)
    return expand_part.astype(jnp.bfloat16), shrink_part.astype(jnp.bfloat16), partial_value


def per_device(
    tokens, out_grad, router_gate, expand_weight, shrink_weight, expert_ids, slot_ids, capacity
):
    tok_dev, width = tokens.shape
    experts = capacity.shape[0]
    slots = max(2, 2 * tok_dev // experts)
    f32, bf16 = jnp.float32, jnp.bfloat16
    table = jnp.arange(experts, dtype=jnp.int32)
    limits = jnp.sum(jnp.where(expert_ids[:, None] == table[None, :], capacity[None, :], 0), axis=1)
    keep = slot_ids < limits
    target = jnp.where(keep, expert_ids * slots + slot_ids, experts * slots)
    place = (jnp.arange(experts * slots, dtype=jnp.int32)[:, None] == target[None, :]).astype(bf16)
    scaled = (router_gate[:, None] * out_grad.astype(f32)).astype(bf16)
    token_send = jnp.dot(place, tokens, preferred_element_type=f32).astype(bf16)
    grad_send = jnp.dot(place, scaled, preferred_element_type=f32).astype(bf16)
    token_send = token_send.reshape(experts, slots, width)
    grad_send = grad_send.reshape(experts, slots, width)
    axes = ("group", "member")
    token_rows = lax.all_to_all(token_send, axes, split_axis=0, concat_axis=0, tiled=True)
    grad_rows = lax.all_to_all(grad_send, axes, split_axis=0, concat_axis=0, tiled=True)
    token_rows = lax.all_gather(token_rows.reshape(-1, width), "pair", axis=0, tiled=True)
    grad_rows = lax.all_gather(grad_rows.reshape(-1, width), "pair", axis=0, tiled=True)
    expand_grad, shrink_grad, partial_value = expert_pass(
        token_rows, grad_rows, expand_weight[0], shrink_weight[0]
    )
    rows = experts * slots
    me = lax.axis_index("pair")
    halves = partial_value.reshape(2, rows, width)
    other = lax.ppermute(
        lax.dynamic_index_in_dim(halves, 1 - me, 0, keepdims=False), "pair", ((0, 1), (1, 0))
    )
    summed = lax.dynamic_index_in_dim(halves, me, 0, keepdims=False) + other
    back = summed.astype(bf16).reshape(experts, slots, width)
    back = lax.all_to_all(back, axes, split_axis=0, concat_axis=0, tiled=True)
    token_grad = lax.dot_general(
        place, back.reshape(rows, width), (((0,), (0,)), ((), ())), preferred_element_type=f32
    ).astype(bf16)
    return (token_grad, expand_grad[None], shrink_grad[None])


def solution(mesh):
    placed = (
        P(("group", "member", "pair"), None),
        P(("group", "member", "pair"), None),
        P(("group", "member", "pair")),
        P(("group", "member"), None, "pair"),
        P(("group", "member"), "pair", None),
        P(("group", "member", "pair")),
        P(("group", "member", "pair")),
        P(),
    )
    return jax.shard_map(
        per_device,
        mesh=mesh,
        in_specs=placed,
        out_specs=(
            P(("group", "member", "pair"), None),
            P(("group", "member"), None, "pair"),
            P(("group", "member"), "pair", None),
        ),
        check_vma=False,
    )
```

time: 167 us -> 103 us (0.62)
  blocking collectives: 52.7 us -> 10.9 us
  between operations: 14.2 us -> 0.81 us
  local copies, waits for them, and re-layouts: 18.5 us -> 5.25 us
  starting transfers between devices: 21.7 us -> 29.9 us
  waiting for transfers between devices: 39.7 us -> 34.7 us
  matrix products: 14.6 us -> 18.2 us
  other arithmetic: 5.33 us -> 3.12 us
    all_to_all x1 -> x0, blocking collectives: 44.8 us -> none  [per_device(): lax.all_to_all(partial_value, ('group', 'member'), split_axis=2, concat_a...]
    all_to_all x2 -> x3, starting transfers between devices: 21.4 us -> 29.5 us  [the longest x1 16.3 us: per_device(): lax.all_to_all(token_send, axes, split_axis=0, concat_axis=0, tiled=True)]
    reduce_scatter x1 -> x0, waiting for transfers between devices: 6.7 us -> none  [per_device(): lax.psum_scatter(returned, 'pair', scatter_dimension=0, tiled=True)]
    all_to_all x3 -> x0, local copies, waits for them, and re-layouts: 4.53 us -> none  [the longest x1 1.67 us: per_device(): lax.all_to_all(grad_both, ('group', 'member'), split_axis=1, concat_axis=...]
    another operation x2 -> x0, local copies, waits for them, and re-layouts: 4.14 us -> none
    dot_general x5 -> x8, matrix products: 14.6 us -> 18.2 us  [the longest x1 4.38 us: expert_pass(): jnp.einsum('rd,rf->df', token_rows, pre_grad, preferred_element_type=f32)]
    all_gather x2 -> x0, local copies, waits for them, and re-layouts: 3.4 us -> none  [the longest x1 1.71 us: per_device(): lax.all_gather(grad_send, 'pair', axis=0, tiled=True)]
    all_gather x2, blocking collectives: 7.89 us -> 10.9 us  [the longest x1 6.43 us: per_device(): lax.all_gather(grad_rows.reshape(-1, width), 'pair', axis=0, tiled=True)]
  transfers between devices with their start and end apart: 3 -> 4, of which waited for: 3 -> 4; matrix products, arithmetic and copies ran while one was open for 10% -> 10% of each run, Pallas kernels for 0% -> 0%
where the time goes in v1:
time: 103 us
  waiting for transfers between devices  34.7 us (34%)
  starting transfers between devices  29.9 us (29%)
  matrix products  18.2 us (18%)
  blocking collectives  10.9 us (11%)
  local copies, waits for them, and re-layouts  5.25 us (5%)
  other arithmetic  3.12 us (3%)
    all_to_all x1, starting transfers between devices, per_device(): lax.all_to_all(token_send, axes, split_axis=0, concat_axis=0, tiled=True)  16.3 us
    all_to_all x1, waiting for transfers between devices, per_device(): lax.all_to_all(token_send, axes, split_axis=0, concat_axis=0, tiled=True)  13.8 us
    all_to_all x1, waiting for transfers between devices, per_device(): lax.all_to_all(grad_send, axes, split_axis=0, concat_axis=0, tiled=True)  9.84 us
    all_to_all x1, waiting for transfers between devices, per_device(): back = lax.all_to_all(back, axes, split_axis=0, concat_axis=0, tiled=True)  8.84 us
    all_to_all x1, starting transfers between devices, per_device(): lax.all_to_all(grad_send, axes, split_axis=0, concat_axis=0, tiled=True)  6.83 us
    all_gather x1, blocking collectives, per_device(): lax.all_gather(grad_rows.reshape(-1, width), 'pair', axis=0, tiled=True)  6.43 us
    all_to_all x1, starting transfers between devices, per_device(): back = lax.all_to_all(back, axes, split_axis=0, concat_axis=0, tiled=True)  6.35 us
    all_gather x1, blocking collectives, per_device(): lax.all_gather(token_rows.reshape(-1, width), 'pair', axis=0, tiled=True)  4.44 us
  transfers between devices with their start and end apart: 4, of which 4 were waited for; matrix products, arithmetic and copies ran while one was open for 10% of the time, Pallas kernels for 0%

profile of v1, /device:TPU:1, one launch (start us, length us, event | category | flops | bytes accessed | tf_op | source)
XLA Modules:
  0.0 102.9 jit_solution(17785780471842416386)
XLA Ops:
  0.6 0.0 copy-start
  0.6 1.0 select_reduce_fusion
  1.6 0.7 compare_select_fusion
  2.3 1.2 %convolution_convert_fusion.2 = bf16[256,768]{1,0:T(8,128)(2,1)S(1)} fusion(bf16[128,768]{1,0:T(8,128)(2,1)} %param.8, s32[128]{0:T(128)S(1)} %compare_select_fusion), kind=kOutput, calls=%fused_computation.24 | convolution fusion | flops 50561024 | bytes 590336 | tf_op jit(solution)/shard_map/dot_general | solution.py:37
  3.5 0.9 reshape.32
  4.4 16.3 %all-to-all-start.1 = ((bf16[128,2,768]{2,1,0:T(2,128)(2,1)}), bf16[128,2,768]{2,1,0:T(2,128)(2,1)S(1)}, u32[]{:S(2)}, u32[]{:S(2)}) async-start(bf16[128,2,768]{2,1,0:T(2,128)(2,1)} %reshape.32), calls=%async_computation.1 | async-start | bytes 786432 | tf_op jit(solution)/shard_map/all_to_all | solution.py:42
  20.7 1.3 %convolution_convert_fusion.3 = bf16[256,768]{1,0:T(8,128)(2,1)S(1)} fusion(bf16[128,768]{1,0:T(8,128)(2,1)} %param.9, f32[128]{0:T(128)} %param.10, s32[128]{0:T(128)S(1)} %compare_select_fusion), kind=kOutput, calls=%fused_computation.25 | convolution fusion | flops 50855936 | bytes 590848 | tf_op jit(solution)/shard_map/dot_general | solution.py:38
  22.0 0.9 reshape.30
  22.9 13.8 %all-to-all-done.1 = bf16[128,2,768]{2,1,0:T(2,128)(2,1)S(1)} async-done(((bf16[128,2,768]{2,1,0:T(2,128)(2,1)}), bf16[128,2,768]{2,1,0:T(2,128)(2,1)S(1)}, u32[]{:S(2)}, u32[]{:S(2)}) %all-to-all-start.1) | async-done | bytes 393248 | tf_op jit(solution)/shard_map/all_to_all | solution.py:42
  36.7 6.8 %all-to-all-start = ((bf16[128,2,768]{2,1,0:T(2,128)(2,1)}), bf16[128,2,768]{2,1,0:T(2,128)(2,1)S(1)}, u32[]{:S(2)}, u32[]{:S(2)}) async-start(bf16[128,2,768]{2,1,0:T(2,128)(2,1)} %reshape.30), calls=%async_computation | async-start | bytes 786432 | tf_op jit(solution)/shard_map/all_to_all | solution.py:43
  43.5 0.1 reshape.33
  43.7 4.4 %all_gather.7 = bf16[512,768]{1,0:T(8,128)(2,1)} all-gather(bf16[256,768]{1,0:T(8,128)(2,1)S(1)} %reshape.33), channel_id=1, replica_groups=mesh['group'=32,'member'=4,'pair'=2] {'pair'}, dimensions={0}, use_global_device_ids=true | all-gather | bytes 1179648 | tf_op jit(solution)/shard_map/all_gather | solution.py:44
  48.1 9.8 %all-to-all-done = bf16[128,2,768]{2,1,0:T(2,128)(2,1)S(1)} async-done(((bf16[128,2,768]{2,1,0:T(2,128)(2,1)}), bf16[128,2,768]{2,1,0:T(2,128)(2,1)S(1)}, u32[]{:S(2)}, u32[]{:S(2)}) %all-to-all-start) | async-done | bytes 393248 | tf_op jit(solution)/shard_map/all_to_all | solution.py:43
  57.9 0.1 reshape.31
  58.1 6.4 %all_gather.6 = bf16[512,768]{1,0:T(8,128)(2,1)S(1)} all-gather(bf16[256,768]{1,0:T(8,128)(2,1)S(1)} %reshape.31), channel_id=1, replica_groups=mesh['group'=32,'member'=4,'pair'=2] {'pair'}, dimensions={0}, use_global_device_ids=true | all-gather | bytes 1179648 | tf_op jit(solution)/shard_map/all_gather | solution.py:45
  64.5 0.0 copy-done
  64.5 0.0 copy-start.3
  64.5 0.0 copy-start.5
  64.5 2.9 %fusion.11 = f32[512,1536]{1,0:T(8,128)S(1)} fusion(bf16[512,768]{1,0:T(8,128)(2,1)} %all_gather.7, bf16[1,768,1536]{2,1,0:T(8,128)(2,1)S(1)} %copy-done), kind=kOutput, calls=%fused_computation.16 | convolution fusion | flops 1207959552 | bytes 6291456 | tf_op jit(solution)/shard_map/rd,df->rf/dot_general | solution.py:13
  67.4 0.0 copy-done.3
  67.4 0.0 copy-done.5
  67.4 0.0 copy-start.7
  67.4 3.1 %fusion.6 = bf16[512,1536]{1,0:T(8,128)(2,1)S(1)} fusion(f32[512,1536]{1,0:T(8,128)S(1)} %fusion.11, bf16[512,768]{1,0:T(8,128)(2,1)S(1)} %all_gather.6, bf16[1,1536,768]{2,1,0:T(8,128)(2,1)S(1)} %copy-done.5), kind=kOutput, calls=%fused_computation.10 | convolution fusion | flops 1223688192 | bytes 7864320 | tf_op jit(solution)/shard_map/rd,fd->rf/dot_general | solution.py:16
  70.5 0.0 copy-done.7
  70.5 0.0 copy-start.6
  70.5 1.4 %fusion.9 = f32[2,256,768]{2,1,0:T(8,128)S(1)} fusion(bf16[2,256,1536]{2,1,0:T(8,128)(2,1)S(1)} %bitcast.30, bf16[1,768,1536]{2,1,0:T(8,128)(2,1)S(1)} %copy-done), kind=kOutput, calls=%fused_computation.14 | convolution fusion | flops 1207959552 | bytes 5505024 | tf_op jit(solution)/shard_map/rf,df->rd/dot_general | solution.py:18
  72.0 0.0 copy-done.6
  72.0 0.0 copy-start.1
  72.0 1.1 %copy-done.1 = f32[2,256,768]{2,1,0:T(8,128)} copy-done((f32[2,256,768]{2,1,0:T(8,128)}, f32[2,256,768]{2,1,0:T(8,128)S(1)}, u32[]{:S(2)}) %copy-start.1) | copy-done | bytes 1572888
  73.1 0.0 copy-start.2
  73.1 0.9 dynamic-slice_bitcast_fusion
  74.0 0.4 collective-permute-start
  74.4 2.3 %collective-permute-done = f32[256,768]{1,0:T(8,128)} collective-permute-done((f32[256,768]{1,0:T(8,128)}, f32[256,768]{1,0:T(8,128)}, u32[]{:S(2)}, u32[]{:S(2)}) %collective-permute-start) | collective-permute-done | bytes 786464 | tf_op jit(solution)/shard_map/ppermute | solution.py:52
  76.7 1.4 %fusion.21 = bf16[256,768]{1,0:T(8,128)(2,1)S(1)} fusion(f32[256,768]{1,0:T(8,128)} %collective-permute-done, f32[2,256,768]{2,1,0:T(8,128)} %copy-done.1, s32[]{:T(128)S(6)} %select_n.17), kind=kLoop, calls=%fused_computation.28 | loop fusion | flops 393216 | bytes 1966084 | tf_op jit(solution)/shard_map/convert_element_type | solution.py:56
  78.1 0.9 reshape.34
  79.0 6.3 %all-to-all-start.2 = ((bf16[128,2,768]{2,1,0:T(2,128)(2,1)}), bf16[128,2,768]{2,1,0:T(2,128)(2,1)S(1)}, u32[]{:S(2)}, u32[]{:S(2)}) async-start(bf16[128,2,768]{2,1,0:T(2,128)(2,1)} %reshape.34), calls=%async_computation.2 | async-start | bytes 786432 | tf_op jit(solution)/shard_map/all_to_all | solution.py:57
  85.4 0.0 copy-done.2
  85.4 0.0 copy-start.4
  85.4 0.0 copy-start.8
  85.4 4.4 %fusion.7 = bf16[1,768,1536]{2,1,0:T(8,128)(2,1)} fusion(bf16[512,768]{1,0:T(8,128)(2,1)S(1)} %copy-done.2, bf16[512,1536]{1,0:T(8,128)(2,1)} %copy-done.6), kind=kOutput, calls=%fused_computation.12 | convolution fusion | flops 1209139200 | bytes 4718592 | tf_op jit(solution)/shard_map/rd,rf->df/dot_general | solution.py:19
  89.8 0.0 copy-done.4
  89.8 0.0 copy-done.8
  89.8 3.2 %fusion.8 = bf16[1,1536,768]{2,1,0:T(8,128)(2,1)} fusion(bf16[512,768]{1,0:T(8,128)(2,1)S(1)} %copy-done.4, f32[512,1536]{1,0:T(8,128)S(1)} %copy-done.8), kind=kOutput, calls=%fused_computation.13 | convolution fusion | flops 1216217088 | bytes 6291456 | tf_op jit(solution)/shard_map/rf,rd->fd/dot_general | solution.py:20
  93.0 8.8 %all-to-all-done.2 = bf16[128,2,768]{2,1,0:T(2,128)(2,1)S(1)} async-done(((bf16[128,2,768]{2,1,0:T(2,128)(2,1)}), bf16[128,2,768]{2,1,0:T(2,128)(2,1)S(1)}, u32[]{:S(2)}, u32[]{:S(2)}) %all-to-all-start.2) | async-done | bytes 393248 | tf_op jit(solution)/shard_map/all_to_all | solution.py:57
  101.8 0.1 reshape.35
  101.9 0.9 convolution_convert_fusion.4
Async XLA Ops:
  0.6 63.9 %copy-start = (bf16[1,768,1536]{2,1,0:T(8,128)(2,1)S(1)}, bf16[1,768,1536]{2,1,0:T(8,128)(2,1)}, u32[]{:S(2)}) copy-start(bf16[1,768,1536]{2,1,0:T(8,128)(2,1)} %param.11) | copy-start | bytes 7077892
  4.4 32.3 %all-to-all-start.1 = ((bf16[128,2,768]{2,1,0:T(2,128)(2,1)}), bf16[128,2,768]{2,1,0:T(2,128)(2,1)S(1)}, u32[]{:S(2)}, u32[]{:S(2)}) async-start(bf16[128,2,768]{2,1,0:T(2,128)(2,1)} %reshape.32), calls=%async_computation.1 | async-start | bytes 786432 | tf_op jit(solution)/shard_map/all_to_all | solution.py:42
  36.7 21.3 %all-to-all-start = ((bf16[128,2,768]{2,1,0:T(2,128)(2,1)}), bf16[128,2,768]{2,1,0:T(2,128)(2,1)S(1)}, u32[]{:S(2)}, u32[]{:S(2)}) async-start(bf16[128,2,768]{2,1,0:T(2,128)(2,1)} %reshape.30), calls=%async_computation | async-start | bytes 786432 | tf_op jit(solution)/shard_map/all_to_all | solution.py:43
  64.5 2.9 %copy-start.3 = (bf16[512,768]{1,0:T(8,128)(2,1)}, bf16[512,768]{1,0:T(8,128)(2,1)S(1)}, u32[]{:S(2)}) copy-start(bf16[512,768]{1,0:T(8,128)(2,1)S(1)} %all_gather.6) | copy-start | bytes 2359300
  64.5 2.9 %copy-start.5 = (bf16[1,1536,768]{2,1,0:T(8,128)(2,1)S(1)}, bf16[1,1536,768]{2,1,0:T(8,128)(2,1)}, u32[]{:S(2)}) copy-start(bf16[1,1536,768]{2,1,0:T(8,128)(2,1)} %param.12) | copy-start | bytes 7077892
  67.4 3.1 %copy-start.7 = (f32[512,1536]{1,0:T(8,128)}, f32[512,1536]{1,0:T(8,128)S(1)}, u32[]{:S(2)}) copy-start(f32[512,1536]{1,0:T(8,128)S(1)} %fusion.11) | copy-start | bytes 9437188
  70.5 1.4 %copy-start.6 = (bf16[512,1536]{1,0:T(8,128)(2,1)}, bf16[512,1536]{1,0:T(8,128)(2,1)S(1)}, u32[]{:S(2)}) copy-start(bf16[512,1536]{1,0:T(8,128)(2,1)S(1)} %fusion.6) | copy-start | bytes 4718596
  72.0 1.1 %copy-start.1 = (f32[2,256,768]{2,1,0:T(8,128)}, f32[2,256,768]{2,1,0:T(8,128)S(1)}, u32[]{:S(2)}) copy-start(f32[2,256,768]{2,1,0:T(8,128)S(1)} %fusion.9) | copy-start | bytes 4718596
  73.1 12.3 %copy-start.2 = (bf16[512,768]{1,0:T(8,128)(2,1)S(1)}, bf16[512,768]{1,0:T(8,128)(2,1)}, u32[]{:S(2)}) copy-start(bf16[512,768]{1,0:T(8,128)(2,1)} %all_gather.7) | copy-start | bytes 2359300
  74.0 2.6 %collective-permute-start = (f32[256,768]{1,0:T(8,128)}, f32[256,768]{1,0:T(8,128)}, u32[]{:S(2)}, u32[]{:S(2)}) collective-permute-start(f32[256,768]{1,0:T(8,128)} %dynamic-slice_bitcast_fusion), channel_id=1, source_target_pairs={{0,1},{1,0},{2,3},{3,2},{4,5},{5,4},{6,7},{7,6},{8,9},{9,8},{10,11... | collective-permute-start | bytes 2359304 | tf_op jit(solution)/shard_map/ppermute | solution.py:52
  79.0 22.8 %all-to-all-start.2 = ((bf16[128,2,768]{2,1,0:T(2,128)(2,1)}), bf16[128,2,768]{2,1,0:T(2,128)(2,1)S(1)}, u32[]{:S(2)}, u32[]{:S(2)}) async-start(bf16[128,2,768]{2,1,0:T(2,128)(2,1)} %reshape.34), calls=%async_computation.2 | async-start | bytes 786432 | tf_op jit(solution)/shard_map/all_to_all | solution.py:57
  85.4 4.4 %copy-start.4 = (bf16[512,768]{1,0:T(8,128)(2,1)S(1)}, bf16[512,768]{1,0:T(8,128)(2,1)}, u32[]{:S(2)}) copy-start(bf16[512,768]{1,0:T(8,128)(2,1)} %copy-done.3) | copy-start | bytes 2359300
  85.4 4.4 %copy-start.8 = (f32[512,1536]{1,0:T(8,128)S(1)}, f32[512,1536]{1,0:T(8,128)}, u32[]{:S(2)}) copy-start(f32[512,1536]{1,0:T(8,128)} %copy-done.7) | copy-start | bytes 9437188

commit v2 on v1

v2 whole, which is shorter than its diff:
```python
import functools

import jax
import jax.numpy as jnp
from jax import lax
from jax.experimental import pallas as pl
from jax.experimental.pallas import tpu as pltpu
from jax.sharding import PartitionSpec as P

MESH = pl.DeviceIdType.MESH
F32 = jnp.float32
BF16 = jnp.bfloat16
CHUNKS = 4
HIDDEN_TILE = 256
GELU_C = 0.7978845608028654
GELU_A = 0.044715
NT = (((1,), (1,)), ((), ()))
TN = (((0,), (0,)), ((), ()))


def dot(a, b, dims=(((1,), (0,)), ((), ()))):
    return lax.dot_general(a, b, dims, preferred_element_type=F32)


def kernel(
    sizes,
    tokens_hbm,
    out_grad_hbm,
    gate_hbm,
    expert_ids_hbm,
    slot_ids_hbm,
    capacity_hbm,
    expand_hbm,
    shrink_hbm,
    token_grad,
    expand_grad,
    shrink_grad,
    tokens,
    out_grad,
    gate,
    expert_ids,
    slot_ids,
    capacity,
    expand,
    shrink,
    place,
    send,
    own,
    other,
    token_rows,
    grad_rows,
    hidden,
    pre_grad,
    partial,
    reduced,
    back_send,
    back,
    back_rows,
    load_sem,
    send_sem,
    recv_sem,
    self_sem,
    pair_send_sem,
    pair_recv_sem,
    sum_send_sem,
    sum_recv_sem,
    back_send_sem,
    back_recv_sem,
):
    nz, nx, ny = sizes
    peers = nz * nx * ny
    tok_dev, width = tokens.shape
    half_ff = expand.shape[1]
    per = peers // CHUNKS
    half = 2 * per
    rows = 2 * half
    group, member, pair = (lax.axis_index(a) for a in ("group", "member", "pair"))
    z, x = lax.div(group, nx), lax.rem(group, nx)
    me = group * ny + member

    def shift(i):
        dz = lax.rem(5 * i, nz)
        q = lax.rem(lax.div(i, nz) + 2 * lax.rem(i, nz), nx * ny)
        return dz, lax.div(q, ny), lax.rem(q, ny)

    def ahead(i):
        dz, dx, dy = shift(i)
        return lax.rem(z + dz, nz) * nx + lax.rem(x + dx, nx), lax.rem(member + dy, ny)

    def behind(i):
        dz, dx, dy = shift(i)
        return (
            lax.rem(z + nz - dz, nz) * nx + lax.rem(x + nx - dx, nx),
            lax.rem(member + ny - dy, ny),
        )

    pairs = (
        (expert_ids_hbm, expert_ids),
        (slot_ids_hbm, slot_ids),
        (capacity_hbm, capacity),
        (gate_hbm, gate),
        (tokens_hbm, tokens),
        (out_grad_hbm, out_grad),
        (expand_hbm, expand),
        (shrink_hbm, shrink),
    )
    loads = [pltpu.make_async_copy(a, b, load_sem.at[n]) for n, (a, b) in enumerate(pairs)]
    for copy in loads:
        copy.start()

    barrier = pltpu.get_barrier_semaphore()
    pl.semaphore_signal(
        barrier, inc=1, device_id=(group, member, 1 - pair), device_id_type=MESH
    )

    @pl.loop(1, peers)
    def _(i):
        g, m = behind(i)
        pl.semaphore_signal(barrier, inc=1, device_id=(g, m, pair), device_id_type=MESH)

    for copy in loads[:6]:
        copy.wait()
    ids, slots = expert_ids[...], slot_ids[...]
    square = (tok_dev, tok_dev)
    down, along = lax.broadcasted_iota(jnp.int32, square, 0), lax.broadcasted_iota(
        jnp.int32, square, 1
    )
    named = jnp.where(lax.broadcasted_iota(jnp.int32, (peers, tok_dev), 0) == ids, 1.0, 0.0)
    limits = dot(
        jnp.broadcast_to(capacity[...].astype(F32), (8, peers)).astype(BF16), named.astype(BF16)
    )[0:1, :]
    target = jnp.where(slots.astype(F32) < limits, 2 * ids + slots, 4 * peers)
    place[...] = jnp.where(
        lax.broadcasted_iota(jnp.int32, (2 * peers, tok_dev), 0) == target, 1.0, 0.0
    ).astype(BF16)
    gates = jnp.sum(jnp.where(down == along, gate[...], 0.0), axis=1, keepdims=True)
    scaled = (gates * out_grad[...].astype(F32)).astype(BF16)
    grad_rows[pl.ds(0, tok_dev), :] = scaled

    @pl.loop(0, 8)
    def _(b):
        block = place[pl.ds(pl.multiple_of(b * (peers // 4), peers // 4), peers // 4), :]
        to = pl.ds(b * (peers // 8), peers // 8)
        shape = (peers // 8, 2, width)
        send[to, 0] = dot(block, tokens[...]).astype(BF16).reshape(shape)
        send[to, 1] = dot(block, grad_rows[pl.ds(0, tok_dev), :]).astype(BF16).reshape(shape)

    pl.semaphore_wait(barrier, peers)
    self_copy = pltpu.make_async_copy(send.at[me], own.at[0], self_sem.at[0])
    self_copy.start()

    for c in range(CHUNKS):

        @pl.loop(max(1, c * per), (c + 1) * per)
        def _(i, c=c):
            g, m = ahead(i)
            pltpu.make_async_remote_copy(
                send.at[g * ny + m],
                own.at[i],
                send_sem,
                recv_sem.at[c],
                device_id=(g, m, pair),
                device_id_type=MESH,
            ).start()

    def pair_copy(c):
        part = pl.ds(c * per, per)
        return pltpu.make_async_remote_copy(
            own.at[part],
            other.at[part],
            pair_send_sem.at[c],
            pair_recv_sem.at[c],
            device_id=(group, member, 1 - pair),
            device_id_type=MESH,
        )

    def sum_copy(c):
        return pltpu.make_async_remote_copy(
            partial.at[c, 1],
            reduced.at[c],
            sum_send_sem.at[c],
            sum_recv_sem.at[c],
            device_id=(group, member, 1 - pair),
            device_id_type=MESH,
        )

    def lay_rows(source, c, at):
        step = 16

        @pl.loop(0, per // step)
        def _(b):
            take = pl.ds(c * per + b * step, step)
            to = pl.ds(pl.multiple_of(c * rows + at + b * 2 * step, 2 * step), 2 * step)
            token_rows[to, :] = source[take, 0].reshape(2 * step, width)
            grad_rows[to, :] = source[take, 1].reshape(2 * step, width)

    def chain(c):
        take = pl.ds(c * rows, rows)

        @pl.loop(0, half_ff // HIDDEN_TILE)
        def _(f):
            tile = pl.ds(pl.multiple_of(f * HIDDEN_TILE, HIDDEN_TILE), HIDDEN_TILE)
            v = dot(token_rows[take, :], expand[:, tile])
            post = dot(grad_rows[take, :], shrink[tile, :], NT)
            square_v = v * v
            t = jnp.tanh(GELU_C * (v + GELU_A * (v * square_v)))
            lower = 0.5 * (1.0 + t)
            hidden[take, tile] = (v * lower).astype(BF16)
            slope = lower + (0.5 * v) * (1.0 - t * t) * (
                GELU_C + (3.0 * GELU_A * GELU_C) * square_v
            )
            pre_grad[take, tile] = (slope * post).astype(BF16)

        @pl.loop(0, width // 256)
        def _(d):
            tile = pl.ds(pl.multiple_of(d * 256, 256), 256)
            value = dot(pre_grad[take, :], expand[tile, :], NT)
            partial[c, 0, :, tile] = value[:half]
            partial[c, 1, :, tile] = value[half:]

    def finish(c):
        sum_copy(c).wait_recv()
        step = 16

        @pl.loop(0, per // step)
        def _(b):
            take = pl.ds(pl.multiple_of(b * 2 * step, 2 * step), 2 * step)
            value = (partial[c, 0, take, :] + reduced[c, take, :]).astype(BF16)
            back_send[pl.ds(c * per + b * step, step)] = value.reshape(step, 2, width)

        if c == 0:
            pltpu.make_async_copy(back_send.at[0], back.at[me], self_sem.at[1]).start()

        @pl.loop(max(1, c * per), (c + 1) * per)
        def _(i):
            g, m = behind(i)
            pltpu.make_async_remote_copy(
                back_send.at[i],
                back.at[me],
                back_send_sem,
                back_recv_sem,
                device_id=(g, m, pair),
                device_id_type=MESH,
            ).start()

    for c in range(CHUNKS):
        if c == 0:
            self_copy.wait()
        landed = own.at[pl.ds(max(1, c * per), per - (c == 0))]
        pltpu.make_async_copy(landed, landed, recv_sem.at[c]).wait()
        pair_copy(c).start()
        lay_rows(own, c, 0)
        if c == 0:
            for copy in loads[6:]:
                copy.wait()
        else:
            finish(c - 1)
        pair_copy(c).wait_recv()
        lay_rows(other, c, half)
        chain(c)
        sum_copy(c).start()
    finish(CHUNKS - 1)

    @pl.loop(0, half_ff // 256)
    def _(f):
        tile = pl.ds(pl.multiple_of(f * 256, 256), 256)
        shrink_grad[tile, :] = dot(hidden[:, tile], grad_rows[...], TN).astype(BF16)

        @pl.loop(0, width // 256)
        def _(d):
            part = pl.ds(pl.multiple_of(d * 256, 256), 256)
            expand_grad[part, tile] = dot(token_rows[:, part], pre_grad[:, tile], TN).astype(BF16)

    returned = back.at[pl.ds(0, peers - 1)]
    pltpu.make_async_copy(returned, returned, back_recv_sem).wait()
    pltpu.make_async_copy(back_send.at[0], back.at[me], self_sem.at[1]).wait()

    @pl.loop(0, peers // 16)
    def _(b):
        to = pl.ds(pl.multiple_of(b * 32, 32), 32)
        back_rows[to, :] = back[pl.ds(b * 16, 16)].reshape(32, width)

    token_grad[...] = dot(place[...], back_rows[...], TN).astype(BF16)

    sent = send.at[pl.ds(0, peers - 1)]
    pltpu.make_async_copy(sent, sent, send_sem).wait()
    pltpu.make_async_copy(returned, returned, back_send_sem).wait()
    for c in range(CHUNKS):
        pair_copy(c).wait_send()
        sum_copy(c).wait_send()


def per_device(
    sizes, tokens, out_grad, router_gate, expand_weight, shrink_weight, expert_ids, slot_ids, capacity
):
    tok_dev, width = tokens.shape
    peers = capacity.shape[0]
    half_ff = expand_weight.shape[2]
    per = peers // CHUNKS
    rows = 4 * peers
    vmem = pl.BlockSpec(memory_space=pltpu.VMEM)
    hbm = pl.BlockSpec(memory_space=pltpu.HBM)
    dma = pltpu.SemaphoreType.DMA
    token_grad, expand_grad, shrink_grad = pl.pallas_call(
        functools.partial(kernel, sizes),
        out_shape=(
            pltpu.VMEM((tok_dev, width), BF16),
            pltpu.VMEM((width, half_ff), BF16),
            pltpu.VMEM((half_ff, width), BF16),
        ),
        in_specs=[hbm] * 8,
        out_specs=(vmem, vmem, vmem),
        scratch_shapes=[
            pltpu.VMEM((tok_dev, width), BF16),
            pltpu.VMEM((tok_dev, width), BF16),
            pltpu.VMEM((1, tok_dev), F32),
            pltpu.VMEM((1, tok_dev), jnp.int32),
            pltpu.VMEM((1, tok_dev), jnp.int32),
            pltpu.VMEM((1, peers), jnp.int32),
            pltpu.VMEM((width, half_ff), BF16),
            pltpu.VMEM((half_ff, width), BF16),
            pltpu.VMEM((2 * peers, tok_dev), BF16),
            pltpu.VMEM((peers, 2, 2, width), BF16),
            pltpu.VMEM((peers, 2, 2, width), BF16),
            pltpu.VMEM((peers, 2, 2, width), BF16),
            pltpu.VMEM((rows, width), BF16),
            pltpu.VMEM((rows, width), BF16),
            pltpu.VMEM((rows, half_ff), BF16),
            pltpu.VMEM((rows, half_ff), BF16),
            pltpu.VMEM((CHUNKS, 2, 2 * per, width), F32),
            pltpu.VMEM((CHUNKS, 2 * per, width), F32),
            pltpu.VMEM((peers, 2, width), BF16),
            pltpu.VMEM((peers, 2, width), BF16),
            pltpu.VMEM((2 * peers, width), BF16),
            dma((8,)),
            dma,
            dma((CHUNKS,)),
            dma((2,)),
            dma((CHUNKS,)),
            dma((CHUNKS,)),
            dma((CHUNKS,)),
            dma((CHUNKS,)),
            dma,
            dma,
        ],
        compiler_params=pltpu.CompilerParams(
            collective_id=0, has_side_effects=True, vmem_limit_bytes=44 << 20
        ),
        name="expert_backward",
    )(
        *(
            pltpu.with_memory_space_constraint(a, pltpu.HBM)
            for a in (
                tokens,
                out_grad,
                router_gate.reshape(1, tok_dev),
                expert_ids.reshape(1, tok_dev),
                slot_ids.reshape(1, tok_dev),
                capacity.reshape(1, peers),
                expand_weight.reshape(width, half_ff),
                shrink_weight.reshape(half_ff, width),
            )
        )
    )
    return token_grad, expand_grad[None], shrink_grad[None]


def solution(mesh):
    group, member, _ = (mesh.shape[a] for a in ("group", "member", "pair"))
    nx = 4
    placed = (
        P(("group", "member", "pair"), None),
        P(("group", "member", "pair"), None),
        P(("group", "member", "pair")),
        P(("group", "member"), None, "pair"),
        P(("group", "member"), "pair", None),
        P(("group", "member", "pair")),
        P(("group", "member", "pair")),
        P(),
    )
    return jax.shard_map(
        functools.partial(per_device, (group // nx, nx, member)),
        mesh=mesh,
        in_specs=placed,
        out_specs=(
            P(("group", "member", "pair"), None),
            P(("group", "member"), None, "pair"),
            P(("group", "member"), "pair", None),
        ),
        check_vma=False,
    )
```

time: 103 us -> 60 us (0.58)
  Pallas kernels: 0 us -> 55.8 us
  waiting for transfers between devices: 34.7 us -> 0 us
  starting transfers between devices: 29.9 us -> 0 us
  matrix products: 18.2 us -> 0 us
  blocking collectives: 10.9 us -> 0 us
  other arithmetic: 3.12 us -> 0 us
  local copies, waits for them, and re-layouts: 5.25 us -> 3.49 us
    pallas_call x0 -> x1, Pallas kernels: none -> 55.8 us  [per_device(): pl.pallas_call(functools.partial(kernel, sizes), out_shape=(pltpu.VMEM((t...]
    all_to_all x3 -> x0, waiting for transfers between devices: 32.4 us -> none  [the longest x1 13.8 us: per_device(): lax.all_to_all(token_send, axes, split_axis=0, concat_axis=0, tiled=True)]
    all_to_all x3 -> x0, starting transfers between devices: 29.5 us -> none  [the longest x1 16.3 us: per_device(): lax.all_to_all(token_send, axes, split_axis=0, concat_axis=0, tiled=True)]
    dot_general x8 -> x0, matrix products: 18.2 us -> none  [the longest x1 4.38 us: expert_pass(): jnp.einsum('rd,rf->df', token_rows, pre_grad, preferred_element_type=f32)]
    all_gather x2 -> x0, blocking collectives: 10.9 us -> none  [the longest x1 6.43 us: per_device(): lax.all_gather(grad_rows.reshape(-1, width), 'pair', axis=0, tiled=True)]
    reshape x6 -> x0, local copies, waits for them, and re-layouts: 3.15 us -> none  [the longest x1 0.91 us: per_device(): back = summed.astype(bf16).reshape(experts, slots, width)]
    unnamed x18 -> x3, local copies, waits for them, and re-layouts: 1.17 us -> 3.49 us
    ppermute x1 -> x0, waiting for transfers between devices: 2.26 us -> none  [per_device(): lax.ppermute(lax.dynamic_index_in_dim(halves, 1 - me, 0, keepdims=False),...]
  transfers between devices with their start and end apart: 4 -> 0, of which waited for: 4 -> 0; matrix products, arithmetic and copies ran while one was open for 10% -> 0% of each run, Pallas kernels for 0% -> 0%
where the time goes in v2:
time: 60 us; the launch traced here: 59.9 us
  Pallas kernels  55.8 us (93%)
  local copies, waits for them, and re-layouts  3.49 us (6%)
  between operations  0.64 us (1%)
    pallas_call x1, Pallas kernels, per_device(): pl.pallas_call(functools.partial(kernel, sizes), out_shape=(pltpu.VMEM((t...  55.8 us
    unnamed x3, local copies, waits for them, and re-layouts  3.49 us

profile of v2, /device:TPU:1, one launch (start us, length us, event | category | flops | bytes accessed | tf_op | source)
XLA Modules:
  0.0 59.9 jit_solution(12788362718746349070)
XLA Ops:
  0.6 55.8 %expert_backward.1 = (bf16[128,768]{1,0:T(8,128)(2,1)S(1)}, bf16[768,1536]{1,0:T(8,128)(2,1)S(1)}, bf16[1536,768]{1,0:T(8,128)(2,1)S(1)}) custom-call(bf16[128,768]{1,0:T(8,128)(2,1)} %tokens_hbm.1, bf16[128,768]{1,0:T(8,128)(2,1)} %out_grad_hbm.1, f32[1,128]{1,0:T(1,128)} %bitcast.12, s32[1,128]{1,0:T(1,128)} %bitcast.13, s32[1,128]{1,0:T(1,128)} %bitcast.14, ...), custom_call_target="tpu_custom_call" | custom-call | tf_op jit(solution)/shard_map/expert_backward/pallas_call | solution.py:304
  56.4 0.7 %copy.14 = bf16[128,768]{1,0:T(8,128)(2,1)} copy(bf16[128,768]{1,0:T(8,128)(2,1)S(1)} %get-tuple-element.9) | data formatting | bytes 393216
  57.1 1.4 %copy.15 = bf16[1,768,1536]{2,1,0:T(8,128)(2,1)} copy(bf16[1,768,1536]{2,1,0:T(8,128)(2,1)S(1)} %bitcast.9) | data formatting | bytes 4718592
  58.5 1.4 %copy.16 = bf16[1,1536,768]{2,1,0:T(8,128)(2,1)} copy(bf16[1,1536,768]{2,1,0:T(8,128)(2,1)S(1)} %bitcast.8) | data formatting | bytes 4718592

commit v3 on v2

--- a/solution.py
+++ b/solution.py
@@ -10,7 +10,7 @@
 MESH = pl.DeviceIdType.MESH
 F32 = jnp.float32
 BF16 = jnp.bfloat16
-CHUNKS = 4
+PARTS = (32, 32, 32, 32)
 HIDDEN_TILE = 256
 GELU_C = 0.7978845608028654
 GELU_A = 0.044715
@@ -71,9 +71,7 @@
     peers = nz * nx * ny
     tok_dev, width = tokens.shape
     half_ff = expand.shape[1]
-    per = peers // CHUNKS
-    half = 2 * per
-    rows = 2 * half
+    first = [sum(PARTS[:c]) for c in range(len(PARTS))]
     group, member, pair = (lax.axis_index(a) for a in ("group", "member", "pair"))
     z, x = lax.div(group, nx), lax.rem(group, nx)
     me = group * ny + member
@@ -149,9 +147,9 @@
     self_copy = pltpu.make_async_copy(send.at[me], own.at[0], self_sem.at[0])
     self_copy.start()
 
-    for c in range(CHUNKS):
-
-        @pl.loop(max(1, c * per), (c + 1) * per)
+    for c, at in enumerate(first):
+
+        @pl.loop(max(1, at), at + PARTS[c])
         def _(i, c=c):
             g, m = ahead(i)
             pltpu.make_async_remote_copy(
@@ -164,7 +162,7 @@
             ).start()
 
     def pair_copy(c):
-        part = pl.ds(c * per, per)
+        part = pl.ds(first[c], PARTS[c])
         return pltpu.make_async_remote_copy(
             own.at[part],
             other.at[part],
@@ -176,8 +174,8 @@
 
     def sum_copy(c):
         return pltpu.make_async_remote_copy(
-            partial.at[c, 1],
-            reduced.at[c],
+            partial.at[1, pl.ds(2 * first[c], 2 * PARTS[c])],
+            reduced.at[pl.ds(2 * first[c], 2 * PARTS[c])],
             sum_send_sem.at[c],
             sum_recv_sem.at[c],
             device_id=(group, member, 1 - pair),
@@ -187,51 +185,48 @@
     def lay_rows(source, c, at):
         step = 16
 
-        @pl.loop(0, per // step)
+        @pl.loop(0, PARTS[c] // step)
         def _(b):
-            take = pl.ds(c * per + b * step, step)
-            to = pl.ds(pl.multiple_of(c * rows + at + b * 2 * step, 2 * step), 2 * step)
+            take = pl.ds(first[c] + b * step, step)
+            to = pl.ds(pl.multiple_of(4 * first[c] + at + b * 2 * step, 2 * step), 2 * step)
             token_rows[to, :] = source[take, 0].reshape(2 * step, width)
             grad_rows[to, :] = source[take, 1].reshape(2 * step, width)
 
     def chain(c):
-        take = pl.ds(c * rows, rows)
-
-        @pl.loop(0, half_ff // HIDDEN_TILE)
-        def _(f):
-            tile = pl.ds(pl.multiple_of(f * HIDDEN_TILE, HIDDEN_TILE), HIDDEN_TILE)
+        half = 2 * PARTS[c]
+        take = pl.ds(4 * first[c], 2 * half)
+        for f in range(0, half_ff, HIDDEN_TILE):
+            tile = pl.ds(f, HIDDEN_TILE)
             v = dot(token_rows[take, :], expand[:, tile])
             post = dot(grad_rows[take, :], shrink[tile, :], NT)
             square_v = v * v
-            t = jnp.tanh(GELU_C * (v + GELU_A * (v * square_v)))
-            lower = 0.5 * (1.0 + t)
+            t = jnp.tanh(v * (GELU_C + (GELU_C * GELU_A) * square_v))
+            lower = 0.5 + 0.5 * t
             hidden[take, tile] = (v * lower).astype(BF16)
-            slope = lower + (0.5 * v) * (1.0 - t * t) * (
-                GELU_C + (3.0 * GELU_A * GELU_C) * square_v
+            slope = lower + v * (1.0 - t * t) * (
+                0.5 * GELU_C + (1.5 * GELU_A * GELU_C) * square_v
             )
             pre_grad[take, tile] = (slope * post).astype(BF16)
-
-        @pl.loop(0, width // 256)
-        def _(d):
-            tile = pl.ds(pl.multiple_of(d * 256, 256), 256)
+        for d in range(0, width, 256):
+            tile = pl.ds(d, 256)
             value = dot(pre_grad[take, :], expand[tile, :], NT)
-            partial[c, 0, :, tile] = value[:half]
-            partial[c, 1, :, tile] = value[half:]
+            partial[0, pl.ds(2 * first[c], half), tile] = value[:half]
+            partial[1, pl.ds(2 * first[c], half), tile] = value[half:]
 
     def finish(c):
         sum_copy(c).wait_recv()
         step = 16
 
-        @pl.loop(0, per // step)
+        @pl.loop(0, PARTS[c] // step)
         def _(b):
-            take = pl.ds(pl.multiple_of(b * 2 * step, 2 * step), 2 * step)
-            value = (partial[c, 0, take, :] + reduced[c, take, :]).astype(BF16)
-            back_send[pl.ds(c * per + b * step, step)] = value.reshape(step, 2, width)
+            take = pl.ds(pl.multiple_of(2 * first[c] + b * 2 * step, 2 * step), 2 * step)
+            value = (partial[0, take, :] + reduced[take, :]).astype(BF16)
+            back_send[pl.ds(first[c] + b * step, step)] = value.reshape(step, 2, width)
 
         if c == 0:
             pltpu.make_async_copy(back_send.at[0], back.at[me], self_sem.at[1]).start()
 
-        @pl.loop(max(1, c * per), (c + 1) * per)
+        @pl.loop(max(1, first[c]), first[c] + PARTS[c])
         def _(i):
             g, m = behind(i)
             pltpu.make_async_remote_copy(
@@ -243,10 +238,10 @@
                 device_id_type=MESH,
             ).start()
 
-    for c in range(CHUNKS):
+    for c in range(len(PARTS)):
         if c == 0:
             self_copy.wait()
-        landed = own.at[pl.ds(max(1, c * per), per - (c == 0))]
+        landed = own.at[pl.ds(max(1, first[c]), PARTS[c] - (c == 0))]
         pltpu.make_async_copy(landed, landed, recv_sem.at[c]).wait()
         pair_copy(c).start()
         lay_rows(own, c, 0)
@@ -256,20 +251,23 @@
         else:
             finish(c - 1)
         pair_copy(c).wait_recv()
-        lay_rows(other, c, half)
+        lay_rows(other, c, 2 * PARTS[c])
         chain(c)
         sum_copy(c).start()
-    finish(CHUNKS - 1)
+    finish(len(PARTS) - 1)
 
     @pl.loop(0, half_ff // 256)
     def _(f):
         tile = pl.ds(pl.multiple_of(f * 256, 256), 256)
         shrink_grad[tile, :] = dot(hidden[:, tile], grad_rows[...], TN).astype(BF16)
 
-        @pl.loop(0, width // 256)
-        def _(d):
-            part = pl.ds(pl.multiple_of(d * 256, 256), 256)
-            expand_grad[part, tile] = dot(token_rows[:, part], pre_grad[:, tile], TN).astype(BF16)
+    @pl.loop(0, width // 256)
+    def _(d):
+        part = pl.ds(pl.multiple_of(d * 256, 256), 256)
+        turned = token_rows[:, part].T
+        for f in range(0, half_ff, 256):
+            tile = pl.ds(f, 256)
+            expand_grad[part, tile] = dot(turned, pre_grad[:, tile]).astype(BF16)
 
     returned = back.at[pl.ds(0, peers - 1)]
     pltpu.make_async_copy(returned, returned, back_recv_sem).wait()
@@ -285,7 +283,7 @@
     sent = send.at[pl.ds(0, peers - 1)]
     pltpu.make_async_copy(sent, sent, send_sem).wait()
     pltpu.make_async_copy(returned, returned, back_send_sem).wait()
-    for c in range(CHUNKS):
+    for c in range(len(PARTS)):
         pair_copy(c).wait_send()
         sum_copy(c).wait_send()
 
@@ -296,7 +294,7 @@
     tok_dev, width = tokens.shape
     peers = capacity.shape[0]
     half_ff = expand_weight.shape[2]
-    per = peers // CHUNKS
+    count = len(PARTS)
     rows = 4 * peers
     vmem = pl.BlockSpec(memory_space=pltpu.VMEM)
     hbm = pl.BlockSpec(memory_space=pltpu.HBM)
@@ -327,19 +325,19 @@
             pltpu.VMEM((rows, width), BF16),
             pltpu.VMEM((rows, half_ff), BF16),
             pltpu.VMEM((rows, half_ff), BF16),
-            pltpu.VMEM((CHUNKS, 2, 2 * per, width), F32),
-            pltpu.VMEM((CHUNKS, 2 * per, width), F32),
+            pltpu.VMEM((2, 2 * peers, width), F32),
+            pltpu.VMEM((2 * peers, width), F32),
             pltpu.VMEM((peers, 2, width), BF16),
             pltpu.VMEM((peers, 2, width), BF16),
             pltpu.VMEM((2 * peers, width), BF16),
             dma((8,)),
             dma,
-            dma((CHUNKS,)),
+            dma((count,)),
             dma((2,)),
-            dma((CHUNKS,)),
-            dma((CHUNKS,)),
-            dma((CHUNKS,)),
-            dma((CHUNKS,)),
+            dma((count,)),
+            dma((count,)),
+            dma((count,)),
+            dma((count,)),
             dma,
             dma,
         ],

time: 60 us -> 55.3 us (0.922)
  Pallas kernels: 55.8 us -> 51.1 us
    pallas_call x1, Pallas kernels: 55.8 us -> 51.1 us  [per_device(): pl.pallas_call(functools.partial(kernel, sizes), out_shape=(pltpu.VMEM((t...]
where the time goes in v3:
time: 55.3 us
  Pallas kernels  51.1 us (92%)
  local copies, waits for them, and re-layouts  3.49 us (6%)
  between operations  0.64 us (1%)
    pallas_call x1, Pallas kernels, per_device(): pl.pallas_call(functools.partial(kernel, sizes), out_shape=(pltpu.VMEM((t...  51.1 us
    unnamed x3, local copies, waits for them, and re-layouts  3.49 us

profile of v3, /device:TPU:1, one launch (start us, length us, event | category | flops | bytes accessed | tf_op | source)
XLA Modules:
  0.0 55.3 jit_solution(6045649473677786945)
XLA Ops:
  0.6 51.1 %expert_backward.1 = (bf16[128,768]{1,0:T(8,128)(2,1)S(1)}, bf16[768,1536]{1,0:T(8,128)(2,1)S(1)}, bf16[1536,768]{1,0:T(8,128)(2,1)S(1)}) custom-call(bf16[128,768]{1,0:T(8,128)(2,1)} %tokens_hbm.1, bf16[128,768]{1,0:T(8,128)(2,1)} %out_grad_hbm.1, f32[1,128]{1,0:T(1,128)} %bitcast.12, s32[1,128]{1,0:T(1,128)} %bitcast.13, s32[1,128]{1,0:T(1,128)} %bitcast.14, ...), custom_call_target="tpu_custom_call" | custom-call | tf_op jit(solution)/shard_map/expert_backward/pallas_call | solution.py:302
  51.8 0.7 %copy.14 = bf16[128,768]{1,0:T(8,128)(2,1)} copy(bf16[128,768]{1,0:T(8,128)(2,1)S(1)} %get-tuple-element.9) | data formatting | bytes 393216
  52.5 1.4 %copy.15 = bf16[1,768,1536]{2,1,0:T(8,128)(2,1)} copy(bf16[1,768,1536]{2,1,0:T(8,128)(2,1)S(1)} %bitcast.9) | data formatting | bytes 4718592
  53.9 1.4 %copy.16 = bf16[1,1536,768]{2,1,0:T(8,128)(2,1)} copy(bf16[1,1536,768]{2,1,0:T(8,128)(2,1)S(1)} %bitcast.8) | data formatting | bytes 4718592

commit v4 on v3

--- a/solution.py
+++ b/solution.py
@@ -71,26 +71,35 @@
     peers = nz * nx * ny
     tok_dev, width = tokens.shape
     half_ff = expand.shape[1]
+    last = len(PARTS) - 1
     first = [sum(PARTS[:c]) for c in range(len(PARTS))]
     group, member, pair = (lax.axis_index(a) for a in ("group", "member", "pair"))
     z, x = lax.div(group, nx), lax.rem(group, nx)
     me = group * ny + member
 
-    def shift(i):
-        dz = lax.rem(5 * i, nz)
-        q = lax.rem(lax.div(i, nz) + 2 * lax.rem(i, nz), nx * ny)
-        return dz, lax.div(q, ny), lax.rem(q, ny)
-
-    def ahead(i):
-        dz, dx, dy = shift(i)
-        return lax.rem(z + dz, nz) * nx + lax.rem(x + dx, nx), lax.rem(member + dy, ny)
-
-    def behind(i):
-        dz, dx, dy = shift(i)
-        return (
-            lax.rem(z + nz - dz, nz) * nx + lax.rem(x + nx - dx, nx),
-            lax.rem(member + ny - dy, ny),
-        )
+    ring = nx * ny
+    xs = [[lax.rem(x + n, nx) for n in range(nx)], [lax.rem(x + nx - n, nx) for n in range(nx)]]
+    ys = [
+        [lax.rem(member + n, ny) for n in range(ny)],
+        [lax.rem(member + ny - n, ny) for n in range(ny)],
+    ]
+
+    def ahead(j, r):
+        zz = lax.rem(z + j + 5 * r % nz, nz)
+        return zz * nx + xs[0][r // ny], ys[0][r % ny]
+
+    def behind(j, r):
+        zz = lax.rem(z + 2 * nz - j - 5 * r % nz, nz)
+        return zz * nx + xs[1][r // ny], ys[1][r % ny]
+
+    def each(start, stop, body):
+        @pl.loop(start // ring, stop // ring)
+        def _(j):
+            for r in range(ring):
+                if r or start:
+                    body(j, r)
+                else:
+                    pl.when(j > 0)(functools.partial(body, j, r))
 
     pairs = (
         (expert_ids_hbm, expert_ids),
@@ -111,10 +120,11 @@
         barrier, inc=1, device_id=(group, member, 1 - pair), device_id_type=MESH
     )
 
-    @pl.loop(1, peers)
-    def _(i):
-        g, m = behind(i)
+    def greet(j, r):
+        g, m = behind(j, r)
         pl.semaphore_signal(barrier, inc=1, device_id=(g, m, pair), device_id_type=MESH)
+
+    each(0, peers, greet)
 
     for copy in loads[:6]:
         copy.wait()
@@ -149,17 +159,18 @@
 
     for c, at in enumerate(first):
 
-        @pl.loop(max(1, at), at + PARTS[c])
-        def _(i, c=c):
-            g, m = ahead(i)
+        def give(j, r, c=c):
+            g, m = ahead(j, r)
             pltpu.make_async_remote_copy(
                 send.at[g * ny + m],
-                own.at[i],
+                own.at[ring * j + r],
                 send_sem,
                 recv_sem.at[c],
                 device_id=(g, m, pair),
                 device_id_type=MESH,
             ).start()
+
+        each(at, at + PARTS[c], give)
 
     def pair_copy(c):
         part = pl.ds(first[c], PARTS[c])
@@ -226,17 +237,18 @@
         if c == 0:
             pltpu.make_async_copy(back_send.at[0], back.at[me], self_sem.at[1]).start()
 
-        @pl.loop(max(1, first[c]), first[c] + PARTS[c])
-        def _(i):
-            g, m = behind(i)
+        def give(j, r):
+            g, m = behind(j, r)
             pltpu.make_async_remote_copy(
-                back_send.at[i],
+                back_send.at[ring * j + r],
                 back.at[me],
                 back_send_sem,
                 back_recv_sem,
                 device_id=(g, m, pair),
                 device_id_type=MESH,
             ).start()
+
+        each(first[c], first[c] + PARTS[c], give)
 
     for c in range(len(PARTS)):
         if c == 0:
@@ -254,7 +266,7 @@
         lay_rows(other, c, 2 * PARTS[c])
         chain(c)
         sum_copy(c).start()
-    finish(len(PARTS) - 1)
+    finish(last)
 
     @pl.loop(0, half_ff // 256)
     def _(f):
@@ -286,6 +298,15 @@
     for c in range(len(PARTS)):
         pair_copy(c).wait_send()
         sum_copy(c).wait_send()
+
+
+def write(*refs):
+    sems = refs[-1]
+    copies = [pltpu.make_async_copy(refs[n], refs[3 + n], sems.at[n]) for n in (2, 1, 0)]
+    for copy in copies:
+        copy.start()
+    for copy in copies:
+        copy.wait()
 
 
 def per_device(
@@ -360,6 +381,16 @@
             )
         )
     )
+    results = (token_grad, expand_grad, shrink_grad)
+    token_grad, expand_grad, shrink_grad = pl.pallas_call(
+        write,
+        out_shape=tuple(pltpu.HBM(a.shape, a.dtype) for a in results),
+        in_specs=[vmem] * 3,
+        out_specs=(hbm,) * 3,
+        scratch_shapes=[dma((3,))],
+        compiler_params=pltpu.CompilerParams(vmem_limit_bytes=16 << 20),
+        name="write_results",
+    )(*(pltpu.with_memory_space_constraint(a, pltpu.VMEM) for a in results))
     return token_grad, expand_grad[None], shrink_grad[None]
 
 

time: 55.3 us -> 52.2 us (0.944)
  local copies, waits for them, and re-layouts: 3.49 us -> 0 us
    unnamed x3 -> x0, local copies, waits for them, and re-layouts: 3.49 us -> none
    pallas_call x0 -> x1, Pallas kernels: none -> 2.26 us  [per_device(): pl.pallas_call(write, out_shape=tuple((pltpu.HBM(a.shape, a.dtype) for a...]
    pallas_call x1, Pallas kernels: 51.1 us -> 49.2 us  [per_device(): pl.pallas_call(functools.partial(kernel, sizes), out_shape=(pltpu.VMEM((t...]
where the time goes in v4:
time: 52.2 us; the launch traced here: 52.1 us
  Pallas kernels  51.4 us (98%)
  between operations  0.64 us (1%)
    pallas_call x1, Pallas kernels, per_device(): pl.pallas_call(functools.partial(kernel, sizes), out_shape=(pltpu.VMEM((t...  49.2 us
    pallas_call x1, Pallas kernels, per_device(): pl.pallas_call(write, out_shape=tuple((pltpu.HBM(a.shape, a.dtype) for a...  2.26 us

profile of v4, /device:TPU:1, one launch (start us, length us, event | category | flops | bytes accessed | tf_op | source)
XLA Modules:
  0.0 52.1 jit_solution(7976902232651106079)
XLA Ops:
  0.6 49.2 %expert_backward.1 = (bf16[128,768]{1,0:T(8,128)(2,1)S(1)}, bf16[768,1536]{1,0:T(8,128)(2,1)S(1)}, bf16[1536,768]{1,0:T(8,128)(2,1)S(1)}) custom-call(bf16[128,768]{1,0:T(8,128)(2,1)} %tokens_hbm.1, bf16[128,768]{1,0:T(8,128)(2,1)} %out_grad_hbm.1, f32[1,128]{1,0:T(1,128)} %bitcast.10, s32[1,128]{1,0:T(1,128)} %bitcast.11, s32[1,128]{1,0:T(1,128)} %bitcast.12, ...), custom_call_target="tpu_custom_call" | custom-call | tf_op jit(solution)/shard_map/expert_backward/pallas_call | solution.py:323
  49.8 2.3 %write_results.1 = (bf16[128,768]{1,0:T(8,128)(2,1)}, bf16[768,1536]{1,0:T(8,128)(2,1)}, bf16[1536,768]{1,0:T(8,128)(2,1)}) custom-call(bf16[128,768]{1,0:T(8,128)(2,1)S(1)} %get-tuple-element.9.refs_0_, bf16[768,1536]{1,0:T(8,128)(2,1)S(1)} %get-tuple-element.10.refs_1_, bf16[1536,768]{1,0:T(8,128)(2,1)S(1)} %get-tuple-element.11.refs_2_), custom_call_target="tpu_custom_call" | custom-call | tf_op jit(solution)/shard_map/write_results/pallas_call | solution.py:385

commit v5 on v4

--- a/solution.py
+++ b/solution.py
@@ -183,12 +183,13 @@
             device_id_type=MESH,
         )
 
-    def sum_copy(c):
+    def sum_copy(c, d):
+        part, tile = pl.ds(2 * first[c], 2 * PARTS[c]), pl.ds(256 * d, 256)
         return pltpu.make_async_remote_copy(
-            partial.at[1, pl.ds(2 * first[c], 2 * PARTS[c])],
-            reduced.at[pl.ds(2 * first[c], 2 * PARTS[c])],
-            sum_send_sem.at[c],
-            sum_recv_sem.at[c],
+            partial.at[1, part, tile],
+            reduced.at[part, tile],
+            sum_send_sem.at[c, d],
+            sum_recv_sem.at[c, d],
             device_id=(group, member, 1 - pair),
             device_id_type=MESH,
         )
@@ -223,9 +224,11 @@
             value = dot(pre_grad[take, :], expand[tile, :], NT)
             partial[0, pl.ds(2 * first[c], half), tile] = value[:half]
             partial[1, pl.ds(2 * first[c], half), tile] = value[half:]
+            sum_copy(c, d // 256).start()
 
     def finish(c):
-        sum_copy(c).wait_recv()
+        for d in range(width // 256):
+            sum_copy(c, d).wait_recv()
         step = 16
 
         @pl.loop(0, PARTS[c] // step)
@@ -265,7 +268,6 @@
         pair_copy(c).wait_recv()
         lay_rows(other, c, 2 * PARTS[c])
         chain(c)
-        sum_copy(c).start()
     finish(last)
 
     @pl.loop(0, half_ff // 256)
@@ -297,7 +299,8 @@
     pltpu.make_async_copy(returned, returned, back_send_sem).wait()
     for c in range(len(PARTS)):
         pair_copy(c).wait_send()
-        sum_copy(c).wait_send()
+        for d in range(width // 256):
+            sum_copy(c, d).wait_send()
 
 
 def write(*refs):
@@ -357,8 +360,8 @@
             dma((2,)),
             dma((count,)),
             dma((count,)),
-            dma((count,)),
-            dma((count,)),
+            dma((count, width // 256)),
+            dma((count, width // 256)),
             dma,
             dma,
         ],

time: 52.2 us -> 53.7 us (1.029)
  Pallas kernels: 51.4 us -> 53 us
    pallas_call x1, Pallas kernels: 49.2 us -> 50.7 us  [per_device(): pl.pallas_call(functools.partial(kernel, sizes), out_shape=(pltpu.VMEM((t...]
where the time goes in v5:
time: 53.7 us; the launch traced here: 53.6 us
  Pallas kernels  53 us (99%)
  between operations  0.64 us (1%)
    pallas_call x1, Pallas kernels, per_device(): pl.pallas_call(functools.partial(kernel, sizes), out_shape=(pltpu.VMEM((t...  50.7 us
    pallas_call x1, Pallas kernels, per_device(): pl.pallas_call(write, out_shape=tuple((pltpu.HBM(a.shape, a.dtype) for a...  2.26 us

profile of v5, /device:TPU:1, one launch (start us, length us, event | category | flops | bytes accessed | tf_op | source)
XLA Modules:
  0.0 53.6 jit_solution(7032042662801725853)
XLA Ops:
  0.6 50.7 %expert_backward.1 = (bf16[128,768]{1,0:T(8,128)(2,1)S(1)}, bf16[768,1536]{1,0:T(8,128)(2,1)S(1)}, bf16[1536,768]{1,0:T(8,128)(2,1)S(1)}) custom-call(bf16[128,768]{1,0:T(8,128)(2,1)} %tokens_hbm.1, bf16[128,768]{1,0:T(8,128)(2,1)} %out_grad_hbm.1, f32[1,128]{1,0:T(1,128)} %bitcast.10, s32[1,128]{1,0:T(1,128)} %bitcast.11, s32[1,128]{1,0:T(1,128)} %bitcast.12, ...), custom_call_target="tpu_custom_call" | custom-call | tf_op jit(solution)/shard_map/expert_backward/pallas_call | solution.py:326
  51.4 2.3 %write_results.1 = (bf16[128,768]{1,0:T(8,128)(2,1)}, bf16[768,1536]{1,0:T(8,128)(2,1)}, bf16[1536,768]{1,0:T(8,128)(2,1)}) custom-call(bf16[128,768]{1,0:T(8,128)(2,1)S(1)} %get-tuple-element.9.refs_0_, bf16[768,1536]{1,0:T(8,128)(2,1)S(1)} %get-tuple-element.10.refs_1_, bf16[1536,768]{1,0:T(8,128)(2,1)S(1)} %get-tuple-element.11.refs_2_), custom_call_target="tpu_custom_call" | custom-call | tf_op jit(solution)/shard_map/write_results/pallas_call | solution.py:388
